TPU v7x, 32 devices: a whole 2x2x4 slice. The times are simulated.
32 devices in a mesh: row: 8 (over z, x), col: 4 (over y, core).
Axes of the slice: x: 2, y: 2, z: 4, core: 2. Of those that a mesh axis runs over, the one named last changes fastest.
Arguments:
- homolog_matrix: bfloat16 [64, 320, 64], P('row', 'col'), may hold values from -6 to 6
- contact_matrix: bfloat16 [320, 320, 128], P('row', 'col'), may hold values from -24 to 24
- genuine_homolog_total: int32 [1], replicated, may hold values from 1 to 64
- genuine_chain_length: int32 [1], replicated, may hold values from 160 to 320
- tensor_product_matrices: bfloat16 [1, 64, 64], replicated, may hold values from -0.75 to 0.75
- tensor_product_final: bfloat16 [1, 1024, 128], replicated, may hold values from -0.75 to 0.75
- mixing_value_gate_matrix: bfloat16 [1, 64, 512], replicated, may hold values from -0.75 to 0.75
- mixing_logit_matrix: bfloat16 [1, 128, 8], replicated
- mixing_final_matrix: bfloat16 [1, 256, 64], replicated, may hold values from -1.5 to 1.5
- feedforward_gate_expand: bfloat16 [1, 128, 1024], replicated, may hold values from -0.5 to 0.5
- feedforward_shrink_matrix: bfloat16 [1, 512, 128], replicated, may hold values from -0.25 to 0.25
Outputs:
- msa_out: bfloat16 [64, 320, 64], P('row', 'col')
- pair_out: bfloat16 [320, 320, 128], P('row', 'col')
Inputs may be any that keep to these rules, and one draw needn't show every extreme that they name: Sequences from genuine_homolog_total on are padding. Residues from genuine_chain_length on are padding.
All inputs are finite; a program needn't handle non-finite values.
Results may differ from a plain program's by a relative error of at most 0.0065.
The roundings to bfloat16 on the way count: a program that leaves them out, or rounds other values in their place, can miss the bound.
Values may be sent and summed in bfloat16 or wider, within the bound.
A program may use at most 64 MiB of HBM per device.

v0:
```python
import jax
import jax.numpy as jnp
from jax import lax
from jax.sharding import PartitionSpec as P

EPSILON = 1e-05
MASKED = -1000000000.0


def broadcast(value, axis, source):
    kept = jnp.where(lax.axis_index(axis) == source, value, 0).astype(value.dtype)
    return lax.psum(kept, axis)


def standardize_features(field):
    field = field.astype(jnp.float32)
    center = field - jnp.mean(field, axis=-1, keepdims=True)
    spread = jnp.mean(center * center, axis=-1, keepdims=True)
    return center * lax.rsqrt(spread + EPSILON)


def local(
    homolog_matrix,
    contact_matrix,
    genuine_homolog_total,
    genuine_chain_length,
    tensor_product_matrices,
    tensor_product_final,
    mixing_value_gate_matrix,
    mixing_logit_matrix,
    mixing_final_matrix,
    feedforward_gate_expand,
    feedforward_shrink_matrix,
):
    homolog_rows_local, chain_positions_local, homolog_rows_full = homolog_matrix.shape
    rows_dev = contact_matrix.shape[0]
    pair_width = contact_matrix.shape[2]
    outer_width = tensor_product_matrices.shape[2] // 2
    head_count = mixing_logit_matrix.shape[2]
    hidden_width = mixing_final_matrix.shape[1]
    head_width = hidden_width // head_count
    trans_width = feedforward_shrink_matrix.shape[1]
    row_blocks = rows_dev // 8
    row_index = lax.axis_index("row")
    col_index = lax.axis_index("col")
    ratio = lax.axis_size("row") // lax.axis_size("col")
    total_seqs = homolog_rows_local * lax.axis_size("row")
    seq_ids = row_index * homolog_rows_local + jnp.arange(homolog_rows_local, dtype=jnp.int32)
    res_ids = col_index * chain_positions_local + jnp.arange(chain_positions_local, dtype=jnp.int32)
    pair_ids = row_index * rows_dev + jnp.arange(rows_dev, dtype=jnp.int32)
    seq_float = (seq_ids < genuine_homolog_total[0]).astype(jnp.float32)
    res_valid = res_ids < genuine_chain_length[0]
    res_float = res_valid.astype(jnp.float32)
    row_float = (pair_ids < genuine_chain_length[0]).astype(jnp.float32)
    divisor = jnp.maximum(
        genuine_homolog_total[0].astype(jnp.float32) * row_float[:, None] * res_float[None, :], 1.0
    )
    starts = jnp.arange(row_blocks, dtype=jnp.int32) * 8
    standardized_source = standardize_features(homolog_matrix).astype(jnp.bfloat16)
    reshaped_tensor = standardized_source.reshape(
        homolog_rows_local * chain_positions_local, homolog_rows_full
    )
    projected = jnp.dot(
        reshaped_tensor, tensor_product_matrices[0], preferred_element_type=jnp.float32
    ).reshape(homolog_rows_local, chain_positions_local, 2 * outer_width)
    projected = (projected * (seq_float[:, None, None] * res_float[None, :, None])).astype(
        jnp.bfloat16
    )
    packed = projected.reshape(homolog_rows_local, chain_positions_local * 2 * outer_width)
    columns = lax.all_gather(packed, "row", axis=0, tiled=True).reshape(
        total_seqs, chain_positions_local, 2 * outer_width
    )
    left_all = columns[:, :, :outer_width].reshape(total_seqs, chain_positions_local * outer_width)
    right = columns[:, :, outer_width:].reshape(total_seqs, chain_positions_local * outer_width)
    left_cols = broadcast(left_all, "col", row_index // ratio).reshape(
        total_seqs, chain_positions_local, outer_width
    )
    left = lax.dynamic_slice_in_dim(left_cols, row_index % ratio * rows_dev, rows_dev, 1)
    outer_weight = tensor_product_final[0]

    def outer_rows(inputs):
        start, pair_rows = inputs
        rows = lax.dynamic_slice_in_dim(left, start, 8, 1).reshape(total_seqs, 8 * outer_width)
        product = lax.dot_general(
            rows, right, (((0,), (0,)), ((), ())), preferred_element_type=jnp.float32
        )
        product = product.reshape(8, outer_width, chain_positions_local, outer_width).transpose(
            0, 2, 1, 3
        )
        product = product.reshape(8, chain_positions_local, outer_width * outer_width)
        scale = lax.dynamic_slice_in_dim(divisor, start, 8, 0)
        outer = (product / scale[:, :, None]).astype(jnp.bfloat16)
        update = jnp.dot(
            outer.reshape(8 * chain_positions_local, outer_width * outer_width),
            outer_weight,
            preferred_element_type=jnp.float32,
        )
        return (
            pair_rows.astype(jnp.float32) + update.reshape(8, chain_positions_local, pair_width)
        ).astype(jnp.bfloat16)

    contact_matrix = lax.map(
        outer_rows,
        (starts, contact_matrix.reshape(row_blocks, 8, chain_positions_local, pair_width)),
    ).reshape(rows_dev, chain_positions_local, pair_width)
    bias_weight = mixing_logit_matrix[0]

    def norm_rows(pair_rows):
        normed_rows = standardize_features(pair_rows).astype(jnp.bfloat16)
        logit_rows = jnp.dot(
            normed_rows.reshape(8 * chain_positions_local, pair_width),
            bias_weight,
            preferred_element_type=jnp.float32,
        )
        return (normed_rows, logit_rows.reshape(8, chain_positions_local, head_count))

    pair_normed, logits = lax.map(
        norm_rows, contact_matrix.reshape(row_blocks, 8, chain_positions_local, pair_width)
    )
    logits = jnp.where(
        res_valid[None, :, None],
        logits.reshape(rows_dev, chain_positions_local, head_count),
        MASKED,
    )
    logits = logits.transpose(0, 2, 1)
    peak = lax.pmax(jnp.max(logits, axis=2), "col")
    expo = jnp.exp(logits - peak[:, :, None])
    totals = lax.psum(jnp.sum(expo, axis=2), "col")
    local_weights = (expo / totals[:, :, None]).astype(jnp.bfloat16)
    part_rows = rows_dev // lax.axis_size("row")
    sectioned = local_weights.reshape(1, rows_dev, head_count, 1, chain_positions_local)
    moved = lax.all_to_all(
        lax.all_to_all(sectioned, "row", split_axis=1, concat_axis=0, tiled=True),
        "col",
        split_axis=0,
        concat_axis=3,
        tiled=True,
    )
    moved = moved.reshape(
        ratio, part_rows, head_count, lax.axis_size("col") * chain_positions_local
    )
    mine = lax.all_gather(moved, "row", axis=1, tiled=True).reshape(
        chain_positions_local, head_count, lax.axis_size("col") * chain_positions_local
    )
    value_weight = mixing_value_gate_matrix[0][:, :hidden_width]
    gate_weight = mixing_value_gate_matrix[0][:, hidden_width:]
    gate = jax.nn.sigmoid(
        jnp.dot(reshaped_tensor, gate_weight, preferred_element_type=jnp.float32)
    ).reshape(homolog_rows_local, chain_positions_local, hidden_width)
    values_local = jnp.dot(reshaped_tensor, value_weight, preferred_element_type=jnp.float32)
    values_local = values_local.astype(jnp.bfloat16).reshape(
        homolog_rows_local, chain_positions_local, hidden_width
    )
    values_piece = lax.all_gather(values_local, "col", axis=1, tiled=True)
    count = values_piece.shape[1]
    heads_piece = values_piece.reshape(homolog_rows_local, count, head_count, head_width)
    averaged = jnp.einsum("ihj,sjhc->sihc", mine, heads_piece, preferred_element_type=jnp.float32)
    gated = (
        gate * averaged.reshape(homolog_rows_local, chain_positions_local, hidden_width)
    ).astype(jnp.bfloat16)
    contact_increment = jnp.dot(
        gated.reshape(homolog_rows_local * chain_positions_local, hidden_width),
        mixing_final_matrix[0],
        preferred_element_type=jnp.float32,
    )
    homolog_matrix = (
        homolog_matrix.astype(jnp.float32)
        + contact_increment.reshape(homolog_rows_local, chain_positions_local, homolog_rows_full)
    ).astype(jnp.bfloat16)
    up_weight = feedforward_gate_expand[0]
    down_weight = feedforward_shrink_matrix[0]

    def transition_rows(inputs):
        pair_rows, normed_rows = inputs
        hidden = jnp.dot(
            normed_rows.reshape(8 * chain_positions_local, pair_width),
            up_weight,
            preferred_element_type=jnp.float32,
        )
        active = (jax.nn.silu(hidden[:, :trans_width]) * hidden[:, trans_width:]).astype(
            jnp.bfloat16
        )
        update = jnp.dot(active, down_weight, preferred_element_type=jnp.float32)
        return (
            pair_rows.astype(jnp.float32) + update.reshape(8, chain_positions_local, pair_width)
        ).astype(jnp.bfloat16)

    contact_matrix = lax.map(
        transition_rows,
        (contact_matrix.reshape(row_blocks, 8, chain_positions_local, pair_width), pair_normed),
    )
    contact_matrix = contact_matrix.reshape(rows_dev, chain_positions_local, pair_width)
    return (homolog_matrix, contact_matrix)


def solution(mesh):
    in_specs = (
        P("row", "col", None),
        P("row", "col", None),
        P(),
        P(),
        P(),
        P(),
        P(),
        P(),
        P(),
        P(),
        P(),
    )
    out_specs = (P("row", "col", None), P("row", "col", None))
    return jax.shard_map(local, mesh=mesh, in_specs=in_specs, out_specs=out_specs, check_vma=False)
```

profile of v0, /device:TPU:0, one launch (start us, length us, event | category | flops | bytes accessed | tf_op | source)
XLA Modules:
  0.0 227.5 jit_solution(14530378645405625014)
XLA Ops:
  8.5 0.9 convert_reduce_fusion.1
  9.5 1.0 fusion.39
  10.5 0.9 fusion.40
  11.5 0.9 fusion.35
  12.8 33.5 %all_gather.10 = bf16[64,5120]{1,0:T(8,128)(2,1)S(1)} all-gather(bf16[8,5120]{1,0:T(8,128)(2,1)S(1)} %reshape.211), channel_id=1, replica_groups=mesh['row'=8,'col'=4] {'row'}, dimensions={0}, use_global_device_ids=true | all-gather | bytes 737280 | tf_op jit(solution)/shard_map/all_gather | solution.py:70
  46.3 0.8 reshape.212
  47.1 1.5 fusion.49
  48.8 0.8 copy.53
  49.8 39.0 %all-reduce.2.cloned.1.call-done = bf16[64,80,32]{2,1,0:T(8,128)(2,1)} async-done(((bf16[64,80,32]{2,1,0:T(8,128)(2,1)}), bf16[64,80,32]{2,1,0:T(8,128)(2,1)}) %all-reduce.2.cloned.1.call-update) | async-done | bytes 327696 | tf_op jit(solution)/shard_map/psum | solution.py:12
  88.9 1.2 constant_dynamic-slice_fusion.2
  90.6 43.2 %while.32 = (s32[]{:T(128)}, bf16[5,8,80,128]{3,2,1,0:T(8,128)(2,1)S(1)}, bf16[5,8,80,128]{3,2,1,0:T(8,128)(2,1)}, s32[5]{0:T(128)S(1)}, bf16[64,40,32]{0,2,1:T(...) while((s32[]{:T(128)}, ...), condition=%wide.region_4.5_spmd, body=%wide.region_3.4_spmd.sunk | while | flops 253214720 | bytes 15736487 | solution.py:102
  94.7 2.4 %copy.73 = f32[8,80,32,32]{1,3,2,0:T(8,128)S(1)} copy(f32[8,80,32,32]{1,2,3,0:T(8,128)S(1)} %convolution_bitcast_fusion.3) | data formatting | bytes 5242880 | tf_op jit(solution)/shard_map/while/body/eval_jaxpr/transpose | solution.py:87
  97.5 1.7 fusion.83
  103.4 2.4 %copy.73 = f32[8,80,32,32]{1,3,2,0:T(8,128)S(1)} copy(f32[8,80,32,32]{1,2,3,0:T(8,128)S(1)} %convolution_bitcast_fusion.3) | data formatting | bytes 5242880 | tf_op jit(solution)/shard_map/while/body/eval_jaxpr/transpose | solution.py:87
  106.1 1.7 fusion.83
  112.0 2.4 %copy.73 = f32[8,80,32,32]{1,3,2,0:T(8,128)S(1)} copy(f32[8,80,32,32]{1,2,3,0:T(8,128)S(1)} %convolution_bitcast_fusion.3) | data formatting | bytes 5242880 | tf_op jit(solution)/shard_map/while/body/eval_jaxpr/transpose | solution.py:87
  114.8 1.7 fusion.83
  120.6 2.4 %copy.73 = f32[8,80,32,32]{1,3,2,0:T(8,128)S(1)} copy(f32[8,80,32,32]{1,2,3,0:T(8,128)S(1)} %convolution_bitcast_fusion.3) | data formatting | bytes 5242880 | tf_op jit(solution)/shard_map/while/body/eval_jaxpr/transpose | solution.py:87
  123.4 1.7 fusion.83
  129.3 2.4 %copy.73 = f32[8,80,32,32]{1,3,2,0:T(8,128)S(1)} copy(f32[8,80,32,32]{1,2,3,0:T(8,128)S(1)} %convolution_bitcast_fusion.3) | data formatting | bytes 5242880 | tf_op jit(solution)/shard_map/while/body/eval_jaxpr/transpose | solution.py:87
  132.0 1.7 fusion.83
  133.9 5.9 %while.33 = (s32[]{:T(128)}, bf16[5,8,80,128]{3,2,1,0:T(8,128)(2,1)S(1)}, f32[5,8,80,8]{2,3,1,0:T(8,128)S(1)}, bf16[5,8,80,128]{3,2,1,0:T(8,128)(2,1)S(1)}, bf16[128,8]{0,1:T(8,128)(2,1)S(1)}, /*index=5*/s32[]{:T(128)}) while((s32[]{:T(128)}, bf16[5,8,80,128]{3,2,1,0:T(8,128)(2,1)S(1)}, f32[5,8,80,8]{2,3,1,0:T(8,128)S(1)}, ...), condition=%wide.region_8.9_spmd, body=%wide.region_5.8_spmd.sunk | while | flops 2458242 | bytes 889425 | solution.py:117
  139.9 10.4 %pmax.7 = f32[40,8]{1,0:T(8,128)S(1)} all-reduce(f32[40,8]{1,0:T(8,128)S(1)} %bitcast_reduce_fusion), channel_id=1, replica_groups=mesh['row'=8,'col'=4] {'col'}, use_global_device_ids=true, to_apply=%region_10.11 | all-reduce | flops 320 | bytes 2560 | tf_op jit(solution)/shard_map/pmax | solution.py:126
  150.5 10.3 %psum.15 = f32[40,8]{1,0:T(8,128)S(1)} all-reduce(f32[40,8]{1,0:T(8,128)S(1)} %fusion.42), channel_id=1, replica_groups=mesh['row'=8,'col'=4] {'col'}, use_global_device_ids=true, to_apply=%region_12.13 | all-reduce | flops 320 | bytes 2560 | tf_op jit(solution)/shard_map/psum | solution.py:128
  161.5 5.6 %all-to-all-start = ((bf16[1,40,8,1,80]{4,2,3,0,1:T(8,128)(2,1)}), bf16[1,40,8,1,80]{4,2,3,0,1:T(8,128)(2,1)}, u32[]{:S(2)}, u32[]{:S(2)}) async-start(bf16[1,40,8,1,80]{4,2,3,0,1:T(8,128)(2,1)} %fusion.43), calls=%async_computation | async-start | bytes 163840 | tf_op jit(solution)/shard_map/all_to_all | solution.py:133
  167.5 0.8 copy.49
  168.4 5.9 %all-to-all-done = bf16[1,40,8,1,80]{4,2,3,0,1:T(8,128)(2,1)} async-done(((bf16[1,40,8,1,80]{4,2,3,0,1:T(8,128)(2,1)}), bf16[1,40,8,1,80]{4,2,3,0,1:T(8,128)(2,1)}, u32[]{:S(2)}, u32[]{:S(2)}) %all-to-all-start) | async-done | bytes 51232 | tf_op jit(solution)/shard_map/all_to_all | solution.py:133
  174.3 3.5 %all-to-all-start.1 = ((bf16[8,5,8,1,80]{4,2,1,3,0:T(8,128)(2,1)}), bf16[8,5,8,1,80]{4,2,1,3,0:T(8,128)(2,1)S(1)}, u32[]{:S(2)}, u32[]{:S(2)}) async-start(bf16[8,5,8,1,80]{4,2,1,3,0:T(8,128)(2,1)} %bitcast.35), calls=%async_computation.1 | async-start | bytes 163840 | tf_op jit(solution)/shard_map/all_to_all | solution.py:132
  177.9 5.4 %while.34 = (s32[]{:T(128)}, bf16[5,8,80,128]{3,2,1,0:T(8,128)(2,1)S(1)}, bf16[5,8,80,128]{3,2,1,0:T(8,128)(2,1)S(1)}, bf16[5,8,80,128]{3,2,1,0:T(8,128)(2,1)S(1...) while((s32[]{:T(128)}, bf16[5,8,80,128]{3,2,1,0:T(8,128)(2,1)S(1)}, ...), condition=%wide.region_14.15_spmd, body=%wide.region_13.14_spmd.sunk | while | flops 253870080 | bytes 7110741 | solution.py:188
  183.5 31.5 %all_gather.11 = bf16[2,40,8,320]{3,2,1,0:T(8,128)(2,1)S(1)} all-gather(bf16[2,5,8,320]{3,2,1,0:T(8,128)(2,1)S(1)} %reshape.217), channel_id=1, replica_groups=mesh['row'=8,'col'=4] {'row'}, dimensions={1}, use_global_device_ids=true | all-gather | bytes 460800 | tf_op jit(solution)/shard_map/all_gather | solution.py:142
  215.1 2.0 copy.50
  219.7 0.9 fusion.36
  (126 shorter events, 29.0 us)
Async XLA Ops:
  7.2 212.0 %copy-start = (bf16[1,256,64]{1,2,0:T(8,128)(2,1)S(1)}, bf16[1,256,64]{1,2,0:T(8,128)(2,1)}, u32[]{:S(2)}) copy-start(bf16[1,256,64]{1,2,0:T(8,128)(2,1)} %param.25) | copy-start | bytes 98308
  7.2 81.7 %all-reduce.2.cloned.1.call-start = ((), (), s32[]{:S(2)}) async-start(), calls=%async_computation.3 | async-start | bytes 2621440 | tf_op jit(solution)/shard_map/psum | solution.py:12
  49.8 40.7 %copy-start.1 = (bf16[1,1024,128]{2,1,0:T(8,128)(2,1)S(1)}, bf16[1,1024,128]{2,1,0:T(8,128)(2,1)}, u32[]{:S(2)}) copy-start(bf16[1,1024,128]{2,1,0:T(8,128)(2,1)} %param.22) | copy-start | bytes 786436
  90.5 43.3 %copy-start.7 = (bf16[1,128,8]{1,2,0:T(8,128)(2,1)S(1)}, bf16[1,128,8]{1,2,0:T(8,128)(2,1)}, u32[]{:S(2)}) copy-start(bf16[1,128,8]{1,2,0:T(8,128)(2,1)} %param.24) | copy-start | bytes 6148
  133.9 33.4 %copy-start.5 = (bf16[1,64,512]{2,1,0:T(8,128)(2,1)S(1)}, bf16[1,64,512]{2,1,0:T(8,128)(2,1)}, u32[]{:S(2)}) copy-start(bf16[1,64,512]{2,1,0:T(8,128)(2,1)} %param.23) | copy-start | bytes 196612
  139.9 38.0 %copy-start.2 = (bf16[1,128,1024]{2,1,0:T(8,128)(2,1)S(1)}, bf16[1,128,1024]{2,1,0:T(8,128)(2,1)}, u32[]{:S(2)}) copy-start(bf16[1,128,1024]{2,1,0:T(8,128)(2,1)} %param.26) | copy-start | bytes 786436
  139.9 38.0 %copy-start.6 = (bf16[1,512,128]{2,1,0:T(8,128)(2,1)S(1)}, bf16[1,512,128]{2,1,0:T(8,128)(2,1)}, u32[]{:S(2)}) copy-start(bf16[1,512,128]{2,1,0:T(8,128)(2,1)} %param.27) | copy-start | bytes 393220
  161.5 12.7 %all-to-all-start = ((bf16[1,40,8,1,80]{4,2,3,0,1:T(8,128)(2,1)}), bf16[1,40,8,1,80]{4,2,3,0,1:T(8,128)(2,1)}, u32[]{:S(2)}, u32[]{:S(2)}) async-start(bf16[1,40,8,1,80]{4,2,3,0,1:T(8,128)(2,1)} %fusion.43), calls=%async_computation | async-start | bytes 163840 | tf_op jit(solution)/shard_map/all_to_all | solution.py:133
  167.2 47.9 %all-gather.2.cloned.1.call-start = ((), (), s32[]{:S(2)}) async-start(), calls=%async_computation.2 | async-start | bytes 1638400 | tf_op jit(solution)/shard_map/all_gather | solution.py:154
  174.3 9.1 %all-to-all-start.1 = ((bf16[8,5,8,1,80]{4,2,1,3,0:T(8,128)(2,1)}), bf16[8,5,8,1,80]{4,2,1,3,0:T(8,128)(2,1)S(1)}, u32[]{:S(2)}, u32[]{:S(2)}) async-start(bf16[8,5,8,1,80]{4,2,1,3,0:T(8,128)(2,1)} %bitcast.35), calls=%async_computation.1 | async-start | bytes 163840 | tf_op jit(solution)/shard_map/all_to_all | solution.py:132
  183.3 33.7 %copy-start.4 = (bf16[5,8,80,128]{3,2,1,0:T(8,128)(2,1)}, bf16[5,8,80,128]{3,2,1,0:T(8,128)(2,1)S(1)}, u32[]{:S(2)}) copy-start(bf16[5,8,80,128]{3,2,1,0:T(8,128)(2,1)S(1)} %get-tuple-element.107) | copy-start | bytes 2457604
  218.8 0.9 copy-start.3
Sparse Core Ops, SparseCore 0:
  48.8 40.0 all-reduce.1
  169.5 19.9 all-gather.1
where the time goes:
time: 228 us; the launch traced here: 227 us
  blocking collectives  85.6 us (38%)
  waiting for transfers between devices  45 us (20%)
  local copies, waits for them, and re-layouts  27.9 us (12%)
  matrix products  21.6 us (9%)
  between operations  15.7 us (7%)
  other arithmetic  11.6 us (5%)
  loops' own time  10.9 us (5%)
  starting transfers between devices  9.17 us (4%)
    psum x1, waiting for transfers between devices, broadcast(): return lax.psum(kept, axis)  39 us
    all_gather x1, blocking collectives, local(): lax.all_gather(packed, 'row', axis=0, tiled=True)  33.5 us
    all_gather x1, blocking collectives, local(): lax.all_gather(moved, 'row', axis=1, tiled=True)  31.5 us
    transpose x5, local copies, waits for them, and re-layouts, outer_rows(): product.reshape(8, outer_width, chain_positions_local, outer_width)  11.9 us
    another operation x1, loops' own time, local(): lax.map(outer_rows, (starts, contact_matrix.reshape(row_blocks, 8, chain_...  10.6 us
    pmax x1, blocking collectives, local(): peak = lax.pmax(jnp.max(logits, axis=2), 'col')  10.4 us
    psum x1, blocking collectives, local(): totals = lax.psum(jnp.sum(expo, axis=2), 'col')  10.3 us
    dot_general x5, matrix products, outer_rows(): jnp.dot(outer.reshape(8 * chain_positions_local, outer_width * outer_widt...  8.51 us
  transfers between devices with their start and end apart: 4, of which 2 were waited for; matrix products, arithmetic and copies ran while one was open for 3% of the time, Pallas kernels for 0%

commit v1 on v0

--- a/solution.py
+++ b/solution.py
@@ -9,7 +9,7 @@
 
 def broadcast(value, axis, source):
     kept = jnp.where(lax.axis_index(axis) == source, value, 0).astype(value.dtype)
-    return lax.psum(kept, axis)
+    return jnp.sum(lax.all_gather(kept, axis), axis=0)
 
 
 def standardize_features(field):

time: 228 us -> 217 us (0.952)
  waiting for transfers between devices: 45 us -> 30.8 us
    psum x1 -> x0, waiting for transfers between devices: 39 us -> none  [broadcast(): return lax.psum(kept, axis)]
    all_gather x0 -> x1, waiting for transfers between devices: none -> 18 us  [broadcast(): return jnp.sum(lax.all_gather(kept, axis), axis=0)]
    all_gather x1, waiting for transfers between devices: 0.02 us -> 6.78 us  [local(): values_piece = lax.all_gather(values_local, 'col', axis=1, tiled=True)]
    select_n x0 -> x2, local copies, waits for them, and re-layouts: none -> 2.77 us  [broadcast(): jnp.where(lax.axis_index(axis) == source, value, 0).astype(value.dtype)]
  transfers between devices with their start and end apart: 4 -> 4, of which waited for: 2 -> 3; matrix products, arithmetic and copies ran while one was open for 3% -> 4% of each run, Pallas kernels for 0% -> 0%
where the time goes in v1:
time: 217 us; the launch traced here: 216 us
  blocking collectives  85.7 us (39%)
  waiting for transfers between devices  30.8 us (14%)
  local copies, waits for them, and re-layouts  29.5 us (14%)
  matrix products  21.6 us (10%)
  between operations  15.7 us (7%)
  other arithmetic  13.2 us (6%)
  loops' own time  10.3 us (5%)
  starting transfers between devices  9.19 us (4%)
    all_gather x1, blocking collectives, local(): lax.all_gather(packed, 'row', axis=0, tiled=True)  33.5 us
    all_gather x1, blocking collectives, local(): lax.all_gather(moved, 'row', axis=1, tiled=True)  31.5 us
    all_gather x1, waiting for transfers between devices, broadcast(): return jnp.sum(lax.all_gather(kept, axis), axis=0)  18 us
    transpose x5, local copies, waits for them, and re-layouts, outer_rows(): product.reshape(8, outer_width, chain_positions_local, outer_width)  11.9 us
    pmax x1, blocking collectives, local(): peak = lax.pmax(jnp.max(logits, axis=2), 'col')  10.5 us
    psum x1, blocking collectives, local(): totals = lax.psum(jnp.sum(expo, axis=2), 'col')  10.3 us
    another operation x1, loops' own time, local(): lax.map(outer_rows, (starts, contact_matrix.reshape(row_blocks, 8, chain_...  9.93 us
    dot_general x5, matrix products, outer_rows(): jnp.dot(outer.reshape(8 * chain_positions_local, outer_width * outer_widt...  8.51 us
  transfers between devices with their start and end apart: 4, of which 3 were waited for; matrix products, arithmetic and copies ran while one was open for 4% of the time, Pallas kernels for 0%

profile of v1, /device:TPU:0, one launch (start us, length us, event | category | flops | bytes accessed | tf_op | source)
XLA Modules:
  0.0 215.9 jit_solution(5196573323671197689)
XLA Ops:
  8.5 0.9 convert_reduce_fusion.1
  9.5 1.0 fusion.39
  10.5 0.9 fusion.40
  11.5 0.9 fusion.35
  12.8 33.5 %all_gather.14 = bf16[64,5120]{1,0:T(8,128)(2,1)S(1)} all-gather(bf16[8,5120]{1,0:T(8,128)(2,1)S(1)} %reshape.221), channel_id=1, replica_groups=mesh['row'=8,'col'=4] {'row'}, dimensions={0}, use_global_device_ids=true | all-gather | bytes 737280 | tf_op jit(solution)/shard_map/all_gather | solution.py:70
  47.1 1.5 fusion.49
  48.6 1.8 copy.73
  50.4 1.0 copy.74
  52.6 18.0 %all-gather.5.cloned.1.call-done = bf16[4,64,2560]{2,1,0:T(8,128)(2,1)} async-done(((bf16[1,64,2560]{2,1,0:T(8,128)(2,1)}), bf16[4,64,2560]{2,1,0:T(8,128)(2,1)}) %all-gather.5.cloned.1.call-update) | async-done | bytes 1310736 | tf_op jit(solution)/shard_map/all_gather | solution.py:12
  70.7 1.5 reduce_sum.59
  73.1 42.1 %while.32 = (s32[]{:T(128)}, bf16[5,8,80,128]{3,2,1,0:T(8,128)(2,1)S(1)}, bf16[5,8,80,128]{3,2,1,0:T(8,128)(2,1)}, s32[5]{0:T(128)S(1)}, bf16[64,40,32]{0,2,1:T(...) while((s32[]{:T(128)}, ...), condition=%wide.region_4.5_spmd, body=%wide.region_3.4_spmd.sunk | while | flops 253214720 | bytes 15736487 | solution.py:102
  77.1 2.4 %copy.95 = f32[8,80,32,32]{1,3,2,0:T(8,128)S(1)} copy(f32[8,80,32,32]{1,2,3,0:T(8,128)S(1)} %convolution_bitcast_fusion.3) | data formatting | bytes 5242880 | tf_op jit(solution)/shard_map/while/body/eval_jaxpr/transpose | solution.py:87
  79.8 1.7 fusion.83
  85.5 2.4 %copy.95 = f32[8,80,32,32]{1,3,2,0:T(8,128)S(1)} copy(f32[8,80,32,32]{1,2,3,0:T(8,128)S(1)} %convolution_bitcast_fusion.3) | data formatting | bytes 5242880 | tf_op jit(solution)/shard_map/while/body/eval_jaxpr/transpose | solution.py:87
  88.3 1.7 fusion.83
  93.9 2.4 %copy.95 = f32[8,80,32,32]{1,3,2,0:T(8,128)S(1)} copy(f32[8,80,32,32]{1,2,3,0:T(8,128)S(1)} %convolution_bitcast_fusion.3) | data formatting | bytes 5242880 | tf_op jit(solution)/shard_map/while/body/eval_jaxpr/transpose | solution.py:87
  96.7 1.7 fusion.83
  102.3 2.4 %copy.95 = f32[8,80,32,32]{1,3,2,0:T(8,128)S(1)} copy(f32[8,80,32,32]{1,2,3,0:T(8,128)S(1)} %convolution_bitcast_fusion.3) | data formatting | bytes 5242880 | tf_op jit(solution)/shard_map/while/body/eval_jaxpr/transpose | solution.py:87
  105.1 1.7 fusion.83
  110.8 2.4 %copy.95 = f32[8,80,32,32]{1,3,2,0:T(8,128)S(1)} copy(f32[8,80,32,32]{1,2,3,0:T(8,128)S(1)} %convolution_bitcast_fusion.3) | data formatting | bytes 5242880 | tf_op jit(solution)/shard_map/while/body/eval_jaxpr/transpose | solution.py:87
  113.5 1.7 fusion.83
  115.4 5.9 %while.33 = (s32[]{:T(128)}, bf16[5,8,80,128]{3,2,1,0:T(8,128)(2,1)S(1)}, f32[5,8,80,8]{2,3,1,0:T(8,128)S(1)}, bf16[5,8,80,128]{3,2,1,0:T(8,128)(2,1)S(1)}, bf16[128,8]{0,1:T(8,128)(2,1)S(1)}, /*index=5*/s32[]{:T(128)}) while((s32[]{:T(128)}, bf16[5,8,80,128]{3,2,1,0:T(8,128)(2,1)S(1)}, f32[5,8,80,8]{2,3,1,0:T(8,128)S(1)}, ...), condition=%wide.region_8.9_spmd, body=%wide.region_5.8_spmd.sunk | while | flops 2458242 | bytes 889425 | solution.py:117
  121.4 10.5 %pmax.7 = f32[40,8]{1,0:T(8,128)S(1)} all-reduce(f32[40,8]{1,0:T(8,128)S(1)} %bitcast_reduce_fusion), channel_id=1, replica_groups=mesh['row'=8,'col'=4] {'col'}, use_global_device_ids=true, to_apply=%region_10.11 | all-reduce | flops 320 | bytes 2560 | tf_op jit(solution)/shard_map/pmax | solution.py:126
  132.1 10.3 %psum.7 = f32[40,8]{1,0:T(8,128)S(1)} all-reduce(f32[40,8]{1,0:T(8,128)S(1)} %fusion.42), channel_id=1, replica_groups=mesh['row'=8,'col'=4] {'col'}, use_global_device_ids=true, to_apply=%region_12.13 | all-reduce | flops 320 | bytes 2560 | tf_op jit(solution)/shard_map/psum | solution.py:128
  143.1 5.6 %all-to-all-start = ((bf16[1,40,8,1,80]{4,2,3,0,1:T(8,128)(2,1)}), bf16[1,40,8,1,80]{4,2,3,0,1:T(8,128)(2,1)}, u32[]{:S(2)}, u32[]{:S(2)}) async-start(bf16[1,40,8,1,80]{4,2,3,0,1:T(8,128)(2,1)} %fusion.43), calls=%async_computation | async-start | bytes 163840 | tf_op jit(solution)/shard_map/all_to_all | solution.py:133
  150.0 5.9 %all-to-all-done = bf16[1,40,8,1,80]{4,2,3,0,1:T(8,128)(2,1)} async-done(((bf16[1,40,8,1,80]{4,2,3,0,1:T(8,128)(2,1)}), bf16[1,40,8,1,80]{4,2,3,0,1:T(8,128)(2,1)}, u32[]{:S(2)}, u32[]{:S(2)}) %all-to-all-start) | async-done | bytes 51232 | tf_op jit(solution)/shard_map/all_to_all | solution.py:133
  155.9 3.5 %all-to-all-start.1 = ((bf16[8,5,8,1,80]{4,2,1,3,0:T(8,128)(2,1)}), bf16[8,5,8,1,80]{4,2,1,3,0:T(8,128)(2,1)S(1)}, u32[]{:S(2)}, u32[]{:S(2)}) async-start(bf16[8,5,8,1,80]{4,2,1,3,0:T(8,128)(2,1)} %bitcast.37), calls=%async_computation.1 | async-start | bytes 163840 | tf_op jit(solution)/shard_map/all_to_all | solution.py:132
  159.5 5.4 %while.34 = (s32[]{:T(128)}, bf16[5,8,80,128]{3,2,1,0:T(8,128)(2,1)S(1)}, bf16[5,8,80,128]{3,2,1,0:T(8,128)(2,1)S(1)}, bf16[5,8,80,128]{3,2,1,0:T(8,128)(2,1)S(1...) while((s32[]{:T(128)}, bf16[5,8,80,128]{3,2,1,0:T(8,128)(2,1)S(1)}, ...), condition=%wide.region_14.15_spmd, body=%wide.region_13.14_spmd.sunk | while | flops 253870080 | bytes 7110741 | solution.py:188
  164.9 6.8 %all-gather.3.cloned.1.call-done = bf16[8,320,256]{2,0,1:T(8,128)(2,1)} async-done(((bf16[8,80,256]{2,0,1:T(8,128)(2,1)}), bf16[8,320,256]{2,0,1:T(8,128)(2,1)}) %all-gather.3.cloned.1.call-update) | async-done | bytes 1310736 | tf_op jit(solution)/shard_map/all_gather | solution.py:154
  171.7 2.0 copy.70
  173.9 31.5 %all_gather.16 = bf16[2,40,8,320]{3,2,1,0:T(8,128)(2,1)S(1)} all-gather(bf16[2,5,8,320]{3,2,1,0:T(8,128)(2,1)S(1)} %reshape.227), channel_id=1, replica_groups=mesh['row'=8,'col'=4] {'row'}, dimensions={1}, use_global_device_ids=true | all-gather | bytes 460800 | tf_op jit(solution)/shard_map/all_gather | solution.py:142
  208.1 0.9 fusion.36
  (129 shorter events, 31.4 us)
Async XLA Ops:
  7.2 200.4 %copy-start = (bf16[1,256,64]{1,2,0:T(8,128)(2,1)S(1)}, bf16[1,256,64]{1,2,0:T(8,128)(2,1)}, u32[]{:S(2)}) copy-start(bf16[1,256,64]{1,2,0:T(8,128)(2,1)} %param.25) | copy-start | bytes 98308
  7.2 63.5 %all-gather.5.cloned.1.call-start = ((), (), s32[]{:S(2)}) async-start(), calls=%async_computation.3 | async-start | bytes 1638400 | tf_op jit(solution)/shard_map/all_gather | solution.py:12
  72.2 1.0 copy-start.1
  73.1 42.2 %copy-start.7 = (bf16[1,128,8]{1,2,0:T(8,128)(2,1)S(1)}, bf16[1,128,8]{1,2,0:T(8,128)(2,1)}, u32[]{:S(2)}) copy-start(bf16[1,128,8]{1,2,0:T(8,128)(2,1)} %param.24) | copy-start | bytes 6148
  115.4 33.4 %copy-start.5 = (bf16[1,64,512]{2,1,0:T(8,128)(2,1)S(1)}, bf16[1,64,512]{2,1,0:T(8,128)(2,1)}, u32[]{:S(2)}) copy-start(bf16[1,64,512]{2,1,0:T(8,128)(2,1)} %param.23) | copy-start | bytes 196612
  121.4 38.1 %copy-start.2 = (bf16[1,128,1024]{2,1,0:T(8,128)(2,1)S(1)}, bf16[1,128,1024]{2,1,0:T(8,128)(2,1)}, u32[]{:S(2)}) copy-start(bf16[1,128,1024]{2,1,0:T(8,128)(2,1)} %param.26) | copy-start | bytes 786436
  121.4 38.1 %copy-start.6 = (bf16[1,512,128]{2,1,0:T(8,128)(2,1)S(1)}, bf16[1,512,128]{2,1,0:T(8,128)(2,1)}, u32[]{:S(2)}) copy-start(bf16[1,512,128]{2,1,0:T(8,128)(2,1)} %param.27) | copy-start | bytes 393220
  143.1 12.8 %all-to-all-start = ((bf16[1,40,8,1,80]{4,2,3,0,1:T(8,128)(2,1)}), bf16[1,40,8,1,80]{4,2,3,0,1:T(8,128)(2,1)}, u32[]{:S(2)}, u32[]{:S(2)}) async-start(bf16[1,40,8,1,80]{4,2,3,0,1:T(8,128)(2,1)} %fusion.43), calls=%async_computation | async-start | bytes 163840 | tf_op jit(solution)/shard_map/all_to_all | solution.py:133
  148.8 22.9 %all-gather.3.cloned.1.call-start = ((), (), s32[]{:S(2)}) async-start(), calls=%async_computation.2 | async-start | bytes 1638400 | tf_op jit(solution)/shard_map/all_gather | solution.py:154
  155.9 17.8 %all-to-all-start.1 = ((bf16[8,5,8,1,80]{4,2,1,3,0:T(8,128)(2,1)}), bf16[8,5,8,1,80]{4,2,1,3,0:T(8,128)(2,1)S(1)}, u32[]{:S(2)}, u32[]{:S(2)}) async-start(bf16[8,5,8,1,80]{4,2,1,3,0:T(8,128)(2,1)} %bitcast.37), calls=%async_computation.1 | async-start | bytes 163840 | tf_op jit(solution)/shard_map/all_to_all | solution.py:132
  164.9 9.0 %copy-start.4 = (bf16[5,8,80,128]{3,2,1,0:T(8,128)(2,1)}, bf16[5,8,80,128]{3,2,1,0:T(8,128)(2,1)S(1)}, u32[]{:S(2)}) copy-start(bf16[5,8,80,128]{3,2,1,0:T(8,128)(2,1)S(1)} %get-tuple-element.107) | copy-start | bytes 2457604
  207.2 0.9 copy-start.3
Sparse Core Ops, SparseCore 0:
  51.5 19.0 all-gather.4
  151.1 20.5 all-gather.2
